TPU v7x, 32 devices: a whole 2x2x4 slice. The times are simulated.
32 devices in a mesh: floor: 4 (over y, x), strip: 8 (over z, core).
Axes of the slice: x: 2, y: 2, z: 4, core: 2. Of those that a mesh axis runs over, the one named last changes fastest.
Arguments:
- density: float32 [4, 4, 512, 2048], P('floor', None, 'strip'), may hold values from 0.2 to 2
- value_field: float32 [4, 4, 512, 2048], P('floor', None, 'strip'), may hold values from -3 to 3
- row_kernel: bfloat16 [512, 512], P('strip'), may hold values from -0.25 to 0.25
- column_kernel: bfloat16 [2048, 2048], replicated, may hold values from -0.125 to 0.125
- type_weight: float32 [4], replicated, may hold values from 0.5 to 2
- crowd_cost: float32 [4], replicated, may hold values from 0.1 to 1
- exit_drain: float32 [4], replicated, may hold values from 0.05 to 0.5
- exit_type: int32 [4, 128], P('floor', 'strip'), may hold values from 0 to 7
- landing_map: int32 [4, 64, 4], P(None, 'strip'), may hold values from 0 to 63, as said below
Outputs:
- final_density: float32 [4, 4, 512, 2048], P('floor', None, 'strip')
- final_value: float32 [4, 4, 512, 2048], P('floor', None, 'strip')
Inputs may be any that keep to these rules, and one draw needn't show every extreme that they name: Each row of landing_map[f] gives a landing's source tile and source face row on floor f and its target tile and target face row on floor f - 1, in the same strip; tiles lie below 16 and face rows below 64, counted within the strip. Every strip of a floor has 8 landings, with distinct sources and distinct targets. `exit_type`: A value below 4 makes the tile an exit target of that occupant type; larger values mark tiles with no target.
All inputs are finite; a program needn't handle non-finite values.
Results may differ from a plain program's by a relative error of at most 0.0026.
Values may be sent and summed in bfloat16 or wider, within the bound.
A program may use at most 128 MiB of HBM per device.

v0:
```python
import functools

import jax
import jax.numpy as jnp
from jax import lax
from jax.experimental import pallas as pl
from jax.experimental.pallas import tpu as pltpu
from jax.sharding import PartitionSpec as P

SUBSTEPS = 4
TILES = 16
LANE = 128
TOP = 8
BLOCK = 512

time_step = 0.2
viscosity = 1.0
exit_reward = 2.0
stair_rate = 0.5

MESH = pl.DeviceIdType.MESH


def kernel(
    strips, floors, landings, types, rows, width,
    dens_hbm, val_hbm, rk_ref, ck_hbm, tw_ref, cc_ref, ed_ref, et_ref, lm_ref,
    dens_out, val_out,
    m_buf, u_buf, ck, rk, crowd_send, crowd_recv, mix_send, mix_recv,
    hm_send, hm_recv, hu_send, hu_recv, out_send, out_recv,
    drain_fac, reward, keep_map, dst_map, faces,
    load_sem, store_sem, rk_ssem, rk_rsem, c_ssem, c_rsem, x_ssem, x_rsem,
    hm_ssem, hm_rsem, hu_ssem, hu_rsem, o_ssem, o_rsem,
):
    me = lax.axis_index("strip")
    floor = lax.axis_index("floor")
    cw = width // strips
    tile_cols = width // TILES
    per = cw // LANE
    inner = pl.ds(TOP, rows)
    cols = pl.ds(LANE, width)

    load_m = pltpu.make_async_copy(dens_hbm.at[0], m_buf.at[0, :, inner, cols], load_sem.at[0])
    load_u = pltpu.make_async_copy(val_hbm.at[0], u_buf.at[0, :, inner, cols], load_sem.at[1])
    load_ck = pltpu.make_async_copy(ck_hbm, ck, load_sem.at[2])
    load_m.start()
    load_u.start()
    load_ck.start()

    barrier = pltpu.get_barrier_semaphore()
    for off in range(1, strips):
        pl.semaphore_signal(barrier, inc=1, device_id={"strip": lax.rem(me + off, strips)}, device_id_type=MESH)

    @pl.when(floor > 0)
    def _():
        pl.semaphore_signal(barrier, inc=1, device_id={"floor": floor - 1}, device_id_type=MESH)

    @pl.when(floor < floors - 1)
    def _():
        pl.semaphore_signal(barrier, inc=1, device_id={"floor": floor + 1}, device_id_type=MESH)

    peers = strips - 1 + jnp.where(floor > 0, 1, 0) + jnp.where(floor < floors - 1, 1, 0)
    pl.semaphore_wait(barrier, peers)

    def to_all(src_of, dst_ref, ssem, rsem):
        for off in range(1, strips):
            dst = lax.rem(me + off, strips)
            pltpu.make_async_remote_copy(
                src_ref=src_of(dst), dst_ref=dst_ref.at[me],
                send_sem=ssem.at[off], recv_sem=rsem.at[off],
                device_id={"strip": dst}, device_id_type=MESH,
            ).start()

    def from_all(src_of, dst_ref, ssem, rsem):
        for off in range(1, strips):
            dst = lax.rem(me + off, strips)
            src = lax.rem(me + strips - off, strips)
            pltpu.make_async_remote_copy(
                src_ref=src_of(dst), dst_ref=dst_ref.at[src],
                send_sem=ssem.at[off], recv_sem=rsem.at[off],
                device_id={"strip": dst}, device_id_type=MESH,
            ).wait()

    def rim_copy(send, recv, ssem, rsem, t, side):
        return pltpu.make_async_remote_copy(
            src_ref=send.at[t, side], dst_ref=recv.at[t, 1 - side],
            send_sem=ssem.at[t, side], recv_sem=rsem.at[t, 1 - side],
            device_id={"strip": me - 1 if side == 0 else me + 1}, device_id_type=MESH,
        )

    def send_rims(buf, send, recv, ssem, rsem, t):
        for k in range(types):
            send[t, 0, k:k + 1, :] = buf[t % 2, k, TOP:TOP + 1, cols]
            send[t, 1, k:k + 1, :] = buf[t % 2, k, TOP + rows - 1:TOP + rows, cols]

        @pl.when(me > 0)
        def _():
            rim_copy(send, recv, ssem, rsem, t, 0).start()

        @pl.when(me < strips - 1)
        def _():
            rim_copy(send, recv, ssem, rsem, t, 1).start()

    def take_rims(buf, send, recv, ssem, rsem, t):
        def own(side):
            at = TOP if side == 0 else TOP + rows - 1
            to = TOP - 1 if side == 0 else TOP + rows
            for k in range(types):
                buf[t % 2, k, to:to + 1, cols] = buf[t % 2, k, at:at + 1, cols]

        def got(side):
            c = rim_copy(send, recv, ssem, rsem, t, side)
            c.wait_send()
            pltpu.make_async_remote_copy(
                src_ref=send.at[t, side], dst_ref=recv.at[t, side],
                send_sem=ssem.at[t, side], recv_sem=rsem.at[t, side],
                device_id={"strip": me - 1 if side == 0 else me + 1}, device_id_type=MESH,
            ).wait_recv()
            to = TOP - 1 if side == 0 else TOP + rows
            for k in range(types):
                buf[t % 2, k, to:to + 1, cols] = recv[t, side, k:k + 1, :]

        pl.when(me > 0)(lambda: got(0))
        pl.when(me == 0)(lambda: own(0))
        pl.when(me < strips - 1)(lambda: got(1))
        pl.when(me == strips - 1)(lambda: own(1))

    def pad_cols(buf, b):
        for k in range(types):
            first = buf[b, k, inner, LANE:2 * LANE]
            last = buf[b, k, inner, width:width + LANE]
            buf[b, k, inner, 0:LANE] = pltpu.roll(first, LANE - 1, 1)
            buf[b, k, inner, width + LANE:width + 2 * LANE] = pltpu.roll(last, 1, 1)

    def crowd_of(t, initial):
        b = t % 2

        @pl.loop(0, strips)
        def _(j):
            for q in range(per):
                start = pl.multiple_of(j * cw + q * LANE, LANE)
                at = pl.ds(pl.multiple_of(start + LANE, LANE), LANE)
                total = None
                if not initial:
                    keep = keep_map[:, pl.ds(start, LANE)]
                    ids = dst_map[:, pl.ds(start, LANE)]
                for k in range(types):
                    v = m_buf[b, k, inner, at]
                    if not initial:
                        add = jnp.zeros_like(v)
                        for l in range(landings):
                            add = jnp.where(ids == l, out_recv[t - 1, k, l:l + 1, :], add)
                        v = v * keep + add
                        m_buf[b, k, inner, at] = v
                    term = tw_ref[k] * v
                    total = term if total is None else total + term
                if t < SUBSTEPS:
                    crowd_send[t, j, :, q * LANE:(q + 1) * LANE] = total.astype(jnp.bfloat16)

    def send_crowd(t):
        to_all(lambda d: crowd_send.at[t, d], crowd_recv.at[t], c_ssem.at[t], c_rsem.at[t])
        crowd_recv[t, me] = crowd_send[t, me]

    def mix(t):
        from_all(lambda d: crowd_send.at[t, d], crowd_recv.at[t], c_ssem.at[t], c_rsem.at[t])
        crowd = crowd_recv[t].reshape(strips * rows, cw)

        @pl.loop(0, strips)
        def _(j):
            mix_send[t, j] = jnp.dot(rk[j], crowd, preferred_element_type=jnp.float32).astype(jnp.bfloat16)

        to_all(lambda d: mix_send.at[t, d], mix_recv.at[t], x_ssem.at[t], x_rsem.at[t])
        mix_recv[t, me] = mix_send[t, me]

    def add_potential(t):
        b = (t + 1) % 2
        from_all(lambda d: mix_send.at[t, d], mix_recv.at[t], x_ssem.at[t], x_rsem.at[t])
        step = 2 * LANE

        @pl.loop(0, width // step)
        def _(n):
            start = pl.multiple_of(n * step, step)
            acc = None
            for s in range(strips):
                d = jnp.dot(mix_recv[t, s], ck[s * cw:(s + 1) * cw, pl.ds(start, step)], preferred_element_type=jnp.float32)
                acc = d if acc is None else acc + d
            at = pl.ds(pl.multiple_of(start + LANE, LANE), step)
            for k in range(types):
                u_buf[b, k, inner, at] = u_buf[b, k, inner, at] + (time_step * cc_ref[k]) * acc

    def stencil(t):
        b, nb = t % 2, (t + 1) % 2

        @pl.loop(0, types * (width // BLOCK))
        def _(i):
            k = lax.div(i, width // BLOCK)
            start = pl.multiple_of(lax.rem(i, width // BLOCK) * BLOCK, BLOCK)
            wide = pl.ds(start, BLOCK + 2 * LANE)
            mid = pl.ds(pl.multiple_of(start + LANE, LANE), BLOCK)
            fac = drain_fac[k, :, pl.ds(start, BLOCK)]
            rew = reward[k, :, pl.ds(start, BLOCK)]
            for r in range(rows // 8):
                lo = TOP + 8 * r
                mw = m_buf[b, k, lo:lo + 8, wide]
                uw = u_buf[b, k, lo:lo + 8, wide]
                span = BLOCK + 2 * LANE
                m = mw[:, LANE:-LANE]
                u = uw[:, LANE:-LANE]
                ml = pltpu.roll(mw, 1, 1)[:, LANE:-LANE]
                mr = pltpu.roll(mw, span - 1, 1)[:, LANE:-LANE]
                ul = pltpu.roll(uw, 1, 1)[:, LANE:-LANE]
                ur = pltpu.roll(uw, span - 1, 1)[:, LANE:-LANE]
                mu = m_buf[b, k, lo - 1:lo + 7, mid]
                md = m_buf[b, k, lo + 1:lo + 9, mid]
                uu = u_buf[b, k, lo - 1:lo + 7, mid]
                ud = u_buf[b, k, lo + 1:lo + 9, mid]
                flux = None
                lap_u = None
                for mn, un in ((mu, uu), (md, ud), (ml, ul), (mr, ur)):
                    d = un - u
                    term = viscosity * (mn - m) + (mn + m) * (0.5 * d)
                    flux = term if flux is None else flux + term
                    lap_u = d if lap_u is None else lap_u + d
                gr = ud - uu
                gc = ur - ul
                drained = (m + time_step * flux) * fac
                m_buf[nb, k, lo:lo + 8, mid] = drained
                for q in range(BLOCK // LANE):
                    faces[(lax.div(start, LANE) + q) * (rows // 8) + r, k] = drained[:, q * LANE:(q + 1) * LANE]
                u_buf[nb, k, lo:lo + 8, mid] = u + (time_step * viscosity) * lap_u - (0.125 * time_step) * (gr * gr + gc * gc) - rew

    def out_copy(t):
        return pltpu.make_async_remote_copy(
            src_ref=out_send.at[t], dst_ref=out_recv.at[t],
            send_sem=o_ssem.at[t], recv_sem=o_rsem.at[t],
            device_id={"floor": floor - 1}, device_id_type=MESH,
        )

    def stairs(t):
        nb = (t + 1) % 2
        for l in range(landings):
            row = lm_ref[floor, l, 1]
            group = lax.div(row, 8)
            hit = eight + 8 * group == row
            face = faces[lm_ref[floor, l, 0] * (rows // 8) + group]
            out_send[t, :, l, :] = stair_rate * jnp.sum(jnp.where(hit, face, 0.0), axis=1)

        @pl.when(floor > 0)
        def _():
            out_copy(t).start()

    def stairs_in(t):
        @pl.when(floor > 0)
        def _():
            out_copy(t).wait_send()

        @pl.when(floor < floors - 1)
        def _():
            out_copy(t).wait_recv()

        @pl.when(floor == floors - 1)
        def _():
            out_recv[t] = jnp.zeros_like(out_recv[t])

    hm = (hm_send, hm_recv, hm_ssem, hm_rsem)
    hu = (hu_send, hu_recv, hu_ssem, hu_rsem)

    load_m.wait()
    crowd_of(0, True)
    send_crowd(0)
    send_rims(m_buf, *hm, 0)
    load_u.wait()
    send_rims(u_buf, *hu, 0)
    to_all(lambda d: rk_ref, rk, rk_ssem, rk_rsem)
    rk[me] = rk_ref[...]

    above = jnp.minimum(floor + 1, floors - 1)
    for tile in range(TILES):
        kind = et_ref[0, tile]
        here = slice(tile * tile_cols, (tile + 1) * tile_cols)
        for k in range(types):
            hit = jnp.where(kind == k, 1.0, 0.0).astype(jnp.float32)
            drain_fac[k, :, here] = jnp.full((8, tile_cols), 1.0 - ed_ref[k] * hit, jnp.float32)
            reward[k, :, here] = jnp.full((8, tile_cols), (time_step * exit_reward) * hit, jnp.float32)

    eight = lax.broadcasted_iota(jnp.int32, (types, 8, LANE), 1)
    row_at = lax.broadcasted_iota(jnp.int32, (rows, LANE), 0)

    @pl.loop(0, TILES)
    def _(tile):
        keep = jnp.ones((rows, LANE), jnp.float32)
        ids = jnp.full((rows, LANE), landings, jnp.int32)
        for l in range(landings):
            src_row = jnp.where(lm_ref[floor, l, 0] == tile, lm_ref[floor, l, 1], -1)
            dst_row = jnp.where(lm_ref[above, l, 2] == tile, lm_ref[above, l, 3], -1)
            keep = jnp.where(row_at == src_row, 1.0 - stair_rate, keep)
            ids = jnp.where(row_at == dst_row, l, ids)
        at = pl.ds(pl.multiple_of(tile * LANE, LANE), LANE)
        keep_map[:, at] = keep
        dst_map[:, at] = ids

    for t in range(SUBSTEPS):
        if t > 0:
            if t == 1:
                load_ck.wait()
            add_potential(t - 1)
            send_rims(u_buf, *hu, t)
            if t >= 2:
                mix(t)
        pad_cols(m_buf, t % 2)
        pad_cols(u_buf, t % 2)
        take_rims(m_buf, *hm, t)
        take_rims(u_buf, *hu, t)
        stencil(t)
        stairs(t)
        stairs_in(t)
        crowd_of(t + 1, False)
        if t + 1 < SUBSTEPS:
            send_crowd(t + 1)
            send_rims(m_buf, *hm, t + 1)
        if t == 0:
            from_all(lambda d: rk_ref, rk, rk_ssem, rk_rsem)
            mix(0)
            mix(1)
    last = SUBSTEPS % 2
    save_m = pltpu.make_async_copy(m_buf.at[last, :, inner, cols], dens_out.at[0], store_sem.at[0])
    save_m.start()
    add_potential(SUBSTEPS - 1)
    save_u = pltpu.make_async_copy(u_buf.at[last, :, inner, cols], val_out.at[0], store_sem.at[1])
    save_u.start()
    save_m.wait()
    save_u.wait()


def solution(mesh):
    strips = mesh.shape["strip"]
    floors = mesh.shape["floor"]

    def local(density, value_field, row_kernel, column_kernel, type_weight, crowd_cost, exit_drain, exit_type, landing_map):
        _, types, rows, width = density.shape
        landings = landing_map.shape[1]
        depth = row_kernel.shape[1]
        cw = width // strips
        n = SUBSTEPS
        any_spec = pl.BlockSpec(memory_space=pl.ANY)
        vmem = pl.BlockSpec(memory_space=pltpu.VMEM)
        smem = pl.BlockSpec(memory_space=pltpu.SMEM)
        f32, bf16 = jnp.float32, jnp.bfloat16
        dma = pltpu.SemaphoreType.DMA
        return pl.pallas_call(
            functools.partial(kernel, strips, floors, landings, types, rows, width),
            out_shape=(
                jax.ShapeDtypeStruct(density.shape, f32),
                jax.ShapeDtypeStruct(value_field.shape, f32),
            ),
            in_specs=[any_spec, any_spec, vmem, any_spec, smem, smem, smem, smem, smem],
            out_specs=(any_spec, any_spec),
            scratch_shapes=[
                pltpu.VMEM((2, types, rows + 2 * TOP, width + 2 * LANE), f32),
                pltpu.VMEM((2, types, rows + 2 * TOP, width + 2 * LANE), f32),
                pltpu.VMEM(column_kernel.shape, bf16),
                pltpu.VMEM((strips, rows, depth), bf16),
                pltpu.VMEM((n, strips, rows, cw), bf16),
                pltpu.VMEM((n, strips, rows, cw), bf16),
                pltpu.VMEM((n, strips, rows, cw), bf16),
                pltpu.VMEM((n, strips, rows, cw), bf16),
                pltpu.VMEM((n, 2, types, width), f32),
                pltpu.VMEM((n, 2, types, width), f32),
                pltpu.VMEM((n, 2, types, width), f32),
                pltpu.VMEM((n, 2, types, width), f32),
                pltpu.VMEM((n, types, landings, LANE), f32),
                pltpu.VMEM((n, types, landings, LANE), f32),
                pltpu.VMEM((types, 8, width), f32),
                pltpu.VMEM((types, 8, width), f32),
                pltpu.VMEM((rows, width), f32),
                pltpu.VMEM((rows, width), jnp.int32),
                pltpu.VMEM((width // LANE * (rows // 8), types, 8, LANE), f32),
                dma((3,)),
                dma((2,)),
                dma((strips,)),
                dma((strips,)),
                dma((n, strips)),
                dma((n, strips)),
                dma((n, strips)),
                dma((n, strips)),
                dma((n, 2)),
                dma((n, 2)),
                dma((n, 2)),
                dma((n, 2)),
                dma((n,)),
                dma((n,)),
            ],
            compiler_params=pltpu.CompilerParams(
                collective_id=0, has_side_effects=True, vmem_limit_bytes=52 * 1024 * 1024
            ),
        )(density, value_field, row_kernel, column_kernel, type_weight, crowd_cost, exit_drain, exit_type, landing_map)

    placed = (
        P("floor", None, "strip", None),
        P("floor", None, "strip", None),
        P("strip", None),
        P(),
        P(),
        P(),
        P(),
        P("floor", "strip"),
        P(None, "strip", None),
    )
    return jax.shard_map(
        local,
        mesh=mesh,
        in_specs=placed,
        out_specs=(P("floor", None, "strip", None), P("floor", None, "strip", None)),
        check_vma=False,
    )
```

profile of v0, /device:TPU:0, one launch (start us, length us, event | category | flops | bytes accessed | tf_op | source)
XLA Modules:
  0.0 127.7 jit_solution(2045942008109357002)
XLA Ops:
  0.6 0.8 copy.11.lm_ref
  1.4 0.0 copy-start
  1.4 0.8 copy-done
  2.3 0.0 copy-start.1
  2.3 0.7 copy-done.1
  2.9 0.0 copy-start.2
  2.9 0.7 copy-done.2
  3.6 0.0 copy-start.3
  3.6 0.7 copy-done.3
  4.2 0.0 copy-start.4
  4.2 0.7 copy-done.4
  4.9 118.2 %shard_map.104 = (f32[1,4,64,2048]{3,2,1,0:T(8,128)}, f32[1,4,64,2048]{3,2,1,0:T(8,128)}) custom-call(f32[1,4,64,2048]{3,2,1,0:T(8,128)} %dens_hbm.1, f32[1,4,64,2048]{3,2,1,0:T(8,128)} %val_hbm.1, bf16[64,512]{1,0:T(8,128)(2,1)S(1)} %copy-done, bf16[2048,2048]{1,0:T(8,128)(2,1)} %ck_hbm.1, f32[4]{0:T(128)S(1)} %copy-done.1, f32[4]{0:T(128)S(1)} %copy-done.2, ...), custom_call_target="tpu_custom_call" | custom-call | tf_op jit(solution)/shard_map/pallas_call | solution.py:349
  123.1 0.0 copy-start.5
  123.1 3.3 %copy.14 = f32[1,4,64,2048]{3,2,1,0:T(8,128)} copy(f32[1,4,64,2048]{3,2,1,0:T(8,128)} %get-tuple-element.4) | data formatting | bytes 4194304
  126.4 0.0 copy-done.5
  126.4 1.3 %copy.15 = f32[1,4,64,2048]{3,2,1,0:T(8,128)} copy(f32[1,4,64,2048]{3,2,1,0:T(8,128)S(1)} %copy-done.5) | data formatting | bytes 4194304
Async XLA Ops:
  1.4 0.8 copy-start
  2.3 0.7 copy-start.1
  2.9 0.7 copy-start.2
  3.6 0.7 copy-start.3
  4.2 0.7 copy-start.4
  123.1 3.3 %copy-start.5 = (f32[1,4,64,2048]{3,2,1,0:T(8,128)S(1)}, f32[1,4,64,2048]{3,2,1,0:T(8,128)}, u32[]{:S(2)}) copy-start(f32[1,4,64,2048]{3,2,1,0:T(8,128)} %get-tuple-element.5) | copy-start | bytes 6291460
where the time goes:
time: 128 us
  Pallas kernels  118 us (92%)
  local copies, waits for them, and re-layouts  8.85 us (7%)
    pallas_call x1, Pallas kernels, local(): pl.pallas_call(functools.partial(kernel, strips, floors, landings, types,...  118 us
    unnamed x15, local copies, waits for them, and re-layouts  8.85 us

commit v1 on v0

--- a/solution.py
+++ b/solution.py
@@ -143,12 +143,21 @@
                 if not initial:
                     keep = keep_map[:, pl.ds(start, LANE)]
                     ids = dst_map[:, pl.ds(start, LANE)]
+                    slot = jnp.maximum(ids, 0)
+                    landed = ids >= 0
                 for k in range(types):
                     v = m_buf[b, k, inner, at]
                     if not initial:
-                        add = jnp.zeros_like(v)
-                        for l in range(landings):
-                            add = jnp.where(ids == l, out_recv[t - 1, k, l:l + 1, :], add)
+                        if landings == 8:
+                            add = jnp.concatenate([
+                                jnp.take_along_axis(out_recv[t - 1, k], slot[r:r + 8], axis=0, mode="promise_in_bounds")
+                                for r in range(0, rows, 8)
+                            ], axis=0)
+                            add = jnp.where(landed, add, 0.0)
+                        else:
+                            add = jnp.zeros_like(v)
+                            for l in range(landings):
+                                add = jnp.where(ids == l, out_recv[t - 1, k, l:l + 1, :], add)
                         v = v * keep + add
                         m_buf[b, k, inner, at] = v
                     term = tw_ref[k] * v
@@ -164,9 +173,8 @@
         from_all(lambda d: crowd_send.at[t, d], crowd_recv.at[t], c_ssem.at[t], c_rsem.at[t])
         crowd = crowd_recv[t].reshape(strips * rows, cw)
 
-        @pl.loop(0, strips)
-        def _(j):
-            mix_send[t, j] = jnp.dot(rk[j], crowd, preferred_element_type=jnp.float32).astype(jnp.bfloat16)
+        mixed = jnp.dot(rk[...].reshape(strips * rows, -1), crowd, preferred_element_type=jnp.float32)
+        mix_send[t] = mixed.astype(jnp.bfloat16).reshape(strips, rows, cw)
 
         to_all(lambda d: mix_send.at[t, d], mix_recv.at[t], x_ssem.at[t], x_rsem.at[t])
         mix_recv[t, me] = mix_send[t, me]
@@ -187,7 +195,7 @@
             for k in range(types):
                 u_buf[b, k, inner, at] = u_buf[b, k, inner, at] + (time_step * cc_ref[k]) * acc
 
-    def stencil(t):
+    def stencil(t, chunks):
         b, nb = t % 2, (t + 1) % 2
 
         @pl.loop(0, types * (width // BLOCK))
@@ -198,7 +206,7 @@
             mid = pl.ds(pl.multiple_of(start + LANE, LANE), BLOCK)
             fac = drain_fac[k, :, pl.ds(start, BLOCK)]
             rew = reward[k, :, pl.ds(start, BLOCK)]
-            for r in range(rows // 8):
+            for r in chunks:
                 lo = TOP + 8 * r
                 mw = m_buf[b, k, lo:lo + 8, wide]
                 uw = u_buf[b, k, lo:lo + 8, wide]
@@ -213,20 +221,20 @@
                 md = m_buf[b, k, lo + 1:lo + 9, mid]
                 uu = u_buf[b, k, lo - 1:lo + 7, mid]
                 ud = u_buf[b, k, lo + 1:lo + 9, mid]
+                low = u - 2.0 * viscosity
                 flux = None
-                lap_u = None
+                rise = None
                 for mn, un in ((mu, uu), (md, ud), (ml, ul), (mr, ur)):
-                    d = un - u
-                    term = viscosity * (mn - m) + (mn + m) * (0.5 * d)
-                    flux = term if flux is None else flux + term
-                    lap_u = d if lap_u is None else lap_u + d
+                    p = un - low
+                    flux = mn * p if flux is None else flux + mn * p
+                    rise = p if rise is None else rise + p
                 gr = ud - uu
                 gc = ur - ul
-                drained = (m + time_step * flux) * fac
+                drained = ((1.0 - 8.0 * viscosity * time_step) * m + (0.5 * time_step) * (flux + m * rise)) * fac
                 m_buf[nb, k, lo:lo + 8, mid] = drained
+                u_buf[nb, k, lo:lo + 8, mid] = u + (time_step * viscosity) * rise - (0.125 * time_step) * (gr * gr + gc * gc) - rew
                 for q in range(BLOCK // LANE):
                     faces[(lax.div(start, LANE) + q) * (rows // 8) + r, k] = drained[:, q * LANE:(q + 1) * LANE]
-                u_buf[nb, k, lo:lo + 8, mid] = u + (time_step * viscosity) * lap_u - (0.125 * time_step) * (gr * gr + gc * gc) - rew
 
     def out_copy(t):
         return pltpu.make_async_remote_copy(
@@ -280,7 +288,7 @@
         for k in range(types):
             hit = jnp.where(kind == k, 1.0, 0.0).astype(jnp.float32)
             drain_fac[k, :, here] = jnp.full((8, tile_cols), 1.0 - ed_ref[k] * hit, jnp.float32)
-            reward[k, :, here] = jnp.full((8, tile_cols), (time_step * exit_reward) * hit, jnp.float32)
+            reward[k, :, here] = jnp.full((8, tile_cols), time_step * exit_reward * hit + 8.0 * viscosity * viscosity * time_step, jnp.float32)
 
     eight = lax.broadcasted_iota(jnp.int32, (types, 8, LANE), 1)
     row_at = lax.broadcasted_iota(jnp.int32, (rows, LANE), 0)
@@ -288,7 +296,7 @@
     @pl.loop(0, TILES)
     def _(tile):
         keep = jnp.ones((rows, LANE), jnp.float32)
-        ids = jnp.full((rows, LANE), landings, jnp.int32)
+        ids = jnp.full((rows, LANE), -1, jnp.int32)
         for l in range(landings):
             src_row = jnp.where(lm_ref[floor, l, 0] == tile, lm_ref[floor, l, 1], -1)
             dst_row = jnp.where(lm_ref[above, l, 2] == tile, lm_ref[above, l, 3], -1)
@@ -304,23 +312,21 @@
                 load_ck.wait()
             add_potential(t - 1)
             send_rims(u_buf, *hu, t)
-            if t >= 2:
-                mix(t)
         pad_cols(m_buf, t % 2)
         pad_cols(u_buf, t % 2)
+        stencil(t, range(1, rows // 8 - 1))
+        if t == 0:
+            from_all(lambda d: rk_ref, rk, rk_ssem, rk_rsem)
+        mix(t)
         take_rims(m_buf, *hm, t)
         take_rims(u_buf, *hu, t)
-        stencil(t)
+        stencil(t, (0, rows // 8 - 1))
         stairs(t)
         stairs_in(t)
         crowd_of(t + 1, False)
         if t + 1 < SUBSTEPS:
             send_crowd(t + 1)
             send_rims(m_buf, *hm, t + 1)
-        if t == 0:
-            from_all(lambda d: rk_ref, rk, rk_ssem, rk_rsem)
-            mix(0)
-            mix(1)
     last = SUBSTEPS % 2
     save_m = pltpu.make_async_copy(m_buf.at[last, :, inner, cols], dens_out.at[0], store_sem.at[0])
     save_m.start()

time: 128 us -> 106 us (0.83)
  Pallas kernels: 118 us -> 95.5 us
    pallas_call x1, Pallas kernels: 118 us -> 95.5 us  [local(): pl.pallas_call(functools.partial(kernel, strips, floors, landings, types,...]
where the time goes in v1:
time: 106 us; the launch traced here: 105 us
  Pallas kernels  95.5 us (90%)
  local copies, waits for them, and re-layouts  8.85 us (8%)
    pallas_call x1, Pallas kernels, local(): pl.pallas_call(functools.partial(kernel, strips, floors, landings, types,...  95.5 us
    unnamed x15, local copies, waits for them, and re-layouts  8.85 us

profile of v1, /device:TPU:0, one launch (start us, length us, event | category | flops | bytes accessed | tf_op | source)
XLA Modules:
  0.0 105.0 jit_solution(10711085187769064615)
XLA Ops:
  0.6 0.8 copy.11.lm_ref
  1.4 0.0 copy-start
  1.4 0.8 copy-done
  2.3 0.0 copy-start.1
  2.3 0.7 copy-done.1
  2.9 0.0 copy-start.2
  2.9 0.7 copy-done.2
  3.6 0.0 copy-start.3
  3.6 0.7 copy-done.3
  4.2 0.0 copy-start.4
  4.2 0.7 copy-done.4
  4.9 95.5 %shard_map.104 = (f32[1,4,64,2048]{3,2,1,0:T(8,128)}, f32[1,4,64,2048]{3,2,1,0:T(8,128)}) custom-call(f32[1,4,64,2048]{3,2,1,0:T(8,128)} %dens_hbm.1, f32[1,4,64,2048]{3,2,1,0:T(8,128)} %val_hbm.1, bf16[64,512]{1,0:T(8,128)(2,1)S(1)} %copy-done, bf16[2048,2048]{1,0:T(8,128)(2,1)} %ck_hbm.1, f32[4]{0:T(128)S(1)} %copy-done.1, f32[4]{0:T(128)S(1)} %copy-done.2, ...), custom_call_target="tpu_custom_call" | custom-call | tf_op jit(solution)/shard_map/pallas_call | solution.py:355
  100.4 0.0 copy-start.5
  100.4 3.3 %copy.14 = f32[1,4,64,2048]{3,2,1,0:T(8,128)} copy(f32[1,4,64,2048]{3,2,1,0:T(8,128)} %get-tuple-element.4) | data formatting | bytes 4194304
  103.7 0.0 copy-done.5
  103.7 1.3 %copy.15 = f32[1,4,64,2048]{3,2,1,0:T(8,128)} copy(f32[1,4,64,2048]{3,2,1,0:T(8,128)S(1)} %copy-done.5) | data formatting | bytes 4194304
Async XLA Ops:
  1.4 0.8 copy-start
  2.3 0.7 copy-start.1
  2.9 0.7 copy-start.2
  3.6 0.7 copy-start.3
  4.2 0.7 copy-start.4
  100.4 3.3 %copy-start.5 = (f32[1,4,64,2048]{3,2,1,0:T(8,128)S(1)}, f32[1,4,64,2048]{3,2,1,0:T(8,128)}, u32[]{:S(2)}) copy-start(f32[1,4,64,2048]{3,2,1,0:T(8,128)} %get-tuple-element.5) | copy-start | bytes 6291460
